TPU v7x, 256 devices: a whole 4x4x8 slice. The times are simulated.
256 devices in a mesh: section: 8 (over y, core), dp: 32 (over z, x).
Axes of the slice: x: 4, y: 4, z: 8, core: 2. Of those that a mesh axis runs over, the one named last changes fastest.
Arguments:
- crop_maps: bfloat16 [32, 4, 2, 8, 8, 640], P('dp'), may hold values from -6 to 6
- target_maps: int32 [32, 4, 2, 8, 8], P('dp'), may hold values 0 or 1
- crop_counts: int32 [32, 4], P('dp'), may hold values from 1 to 2, as said below
- depth_kernels: float32 [8, 49, 640], P('section'), may hold values from -0.875 to 0.875
- weight_in: bfloat16 [8, 640, 2560], P('section', 'dp'), may hold values from -0.25 to 0.25
- weight_out: bfloat16 [8, 2560, 640], P('section', 'dp'), may hold values from -0.125 to 0.125
- head_weight: float32 [640], replicated, may hold values from -0.25 to 0.25
Outputs:
- grad_in: float32 [8, 640, 2560], P('section', 'dp')
- grad_out: float32 [8, 2560, 640], P('section', 'dp')
- grad_kernels: float32 [8, 49, 640], P('section')
- grad_head: float32 [640], replicated
- loss_value: float32 [], replicated
Inputs may be any that keep to these rules, and one draw needn't show every extreme that they name: `crop_counts`: every data group has some micro-batch with exactly 2 crops.
All inputs are finite; a program needn't handle non-finite values. No bound on the sum of `target_maps` on one device may be relied on, other than what follows from the above.
Results may differ from a plain program's by a relative error of at most 0.034.
Values may be sent and summed in bfloat16 or wider, within the bound.
No kernel may reach another device: no remote copies, remote signals or barrier semaphores. Data moves between devices by JAX's collectives and lax.ppermute only.
A program may use at most 128 MiB of HBM per device.

v0:
```python
import jax
import jax.numpy as jnp
from jax import lax
from jax.sharding import PartitionSpec as P

EPSILON = 1e-06
SQRT_HALF = 0.7071067811865476
INV_ROOT_TWO_PI = 0.3989422804014327


def from_behind(value, axis, steps):
    count = lax.axis_size(axis)
    first, last = (max(0, -steps), min(count, count - steps))
    return lax.ppermute(value, axis, [(source, source + steps) for source in range(first, last)])


def depthwise(values, kernel):
    side = values.shape[1]
    padded = jnp.pad(values, ((0, 0), (3, 3), (3, 3), (0, 0)))
    result = jnp.zeros_like(values)
    for vertical in range(7):
        for across in range(7):
            result = (
                result
                + padded[:, vertical : vertical + side, across : across + side, :]
                * kernel[vertical * 7 + across]
            )
    return result


def depthwise_back(grads, kernel):
    side = grads.shape[1]
    padded = jnp.pad(grads, ((0, 0), (3, 3), (3, 3), (0, 0)))
    result = jnp.zeros_like(grads)
    for vertical in range(7):
        for across in range(7):
            result = (
                result
                + padded[:, 6 - vertical : 6 - vertical + side, 6 - across : 6 - across + side, :]
                * kernel[vertical * 7 + across]
            )
    return result


def kernel_grad(values, grads):
    side = values.shape[1]
    padded = jnp.pad(values, ((0, 0), (3, 3), (3, 3), (0, 0)))
    taps = []
    for vertical in range(7):
        for across in range(7):
            taps.append(
                jnp.sum(
                    padded[:, vertical : vertical + side, across : across + side, :] * grads,
                    axis=(0, 1, 2),
                )
            )
    return jnp.stack(taps, axis=0)


def block_parts(tiles, kernel, weight_in):
    width = tiles.shape[-1]
    widened = tiles.astype(jnp.float32)
    mixed = depthwise(widened, kernel).reshape(-1, width)
    centred = mixed - jnp.mean(mixed, axis=-1, keepdims=True)
    inverse = lax.rsqrt(jnp.mean(centred * centred, axis=-1, keepdims=True) + EPSILON)
    normed = centred * inverse
    normed_low = normed.astype(jnp.bfloat16)
    hidden = jnp.dot(normed_low, weight_in, preferred_element_type=jnp.float32)
    activated = (hidden * 0.5 * (1.0 + lax.erf(hidden * SQRT_HALF))).astype(jnp.bfloat16)
    return (widened, normed, inverse, normed_low, hidden, activated)


def block_forward(tiles, kernel, weight_in, weight_out):
    width = tiles.shape[-1]
    widened, normed, inverse, normed_low, hidden, activated = block_parts(tiles, kernel, weight_in)
    output = jnp.dot(activated, weight_out, preferred_element_type=jnp.float32)
    return (widened.reshape(-1, width) + output).astype(jnp.bfloat16).reshape(tiles.shape)


def block_backward(tiles, upstream, kernel, weight_in, weight_out):
    width = tiles.shape[-1]
    widened, normed, inverse, normed_low, hidden, activated = block_parts(tiles, kernel, weight_in)
    up_flat = upstream.reshape(-1, width)
    through = lax.dot_general(
        up_flat, weight_out, (((1,), (1,)), ((), ())), preferred_element_type=jnp.float32
    )
    slope = (
        0.5 * (1.0 + lax.erf(hidden * SQRT_HALF))
        + hidden * jnp.exp(-0.5 * hidden * hidden) * INV_ROOT_TWO_PI
    )
    hidden_grad = (through * slope).astype(jnp.bfloat16)
    normed_grad = lax.dot_general(
        hidden_grad, weight_in, (((1,), (1,)), ((), ())), preferred_element_type=jnp.float32
    )
    mixed_grad = inverse * (
        normed_grad
        - jnp.mean(normed_grad, axis=-1, keepdims=True)
        - normed * jnp.mean(normed_grad * normed, axis=-1, keepdims=True)
    )
    mixed_tiles = mixed_grad.reshape(tiles.shape)
    kernel_term = kernel_grad(widened, mixed_tiles)
    tile_grad = (upstream.astype(jnp.float32) + depthwise_back(mixed_tiles, kernel)).astype(
        jnp.bfloat16
    )
    return (tile_grad, kernel_term, normed_low, hidden_grad, activated, up_flat)


def outer_sum(left, right):
    return lax.dot_general(
        left, right, (((0,), (0,)), ((), ())), preferred_element_type=jnp.float32
    )


def head_terms(final, targets, live, head_weight, factor):
    widened = final.astype(jnp.float32)
    logits = jnp.sum(widened * head_weight, axis=-1)
    weight_live = live.astype(jnp.float32)[:, :, None, None]
    truth = targets.astype(jnp.float32)
    loss_term = jnp.sum(weight_live * (jax.nn.softplus(logits) - truth * logits)) * factor
    logit_grad = (jax.nn.sigmoid(logits) - truth) * weight_live * factor
    seeds = (logit_grad[..., None] * head_weight).astype(jnp.bfloat16)
    head_term = jnp.sum(logit_grad[..., None] * widened, axis=(0, 1, 2, 3))
    return (loss_term, seeds, head_term)


def body(crop_maps, target_maps, crop_counts, depth_kernels, weight_in, weight_out, head_weight):
    section_index = lax.axis_index("section")
    section_count = lax.axis_size("section")
    micro_count = crop_maps.shape[1]
    slot_count = crop_maps.shape[2]
    kernel = depth_kernels[0]
    live = jnp.arange(slot_count)[None, :] < crop_counts[0][:, None]
    entering = crop_maps[0] * live[:, :, None, None, None].astype(jnp.bfloat16)
    first_full, second_full = (
        lax.all_gather(weight_in[0], "dp", axis=0, tiled=True),
        lax.all_gather(weight_out[0], "dp", axis=0, tiled=True),
    )
    blank_tile = jnp.zeros(entering.shape[1:], jnp.bfloat16)
    ticks = micro_count + section_count - 1

    def forward_step(moment, carry):
        arrived, saved, final = carry
        micro = moment - section_index
        active = (micro >= 0) & (micro < micro_count)
        place = jnp.clip(micro, 0, micro_count - 1)
        own_tiles = lax.dynamic_index_in_dim(entering, place, 0, keepdims=False)
        current = jnp.where(section_index == 0, own_tiles, arrived)
        result = lax.cond(
            active,
            lambda tiles: block_forward(tiles, kernel, first_full, second_full),
            lambda tiles: jnp.zeros_like(tiles),
            current,
        )
        old_saved = lax.dynamic_index_in_dim(saved, place, 0, keepdims=False)
        saved = lax.dynamic_update_index_in_dim(
            saved, jnp.where(active, current, old_saved), place, 0
        )
        old_final = lax.dynamic_index_in_dim(final, place, 0, keepdims=False)
        final = lax.dynamic_update_index_in_dim(
            final, jnp.where(active, result, old_final), place, 0
        )
        arrived = from_behind(result, "section", 1)
        return (arrived, saved, final)

    _, saved, final = lax.fori_loop(
        0, ticks, forward_step, (blank_tile, jnp.zeros_like(entering), jnp.zeros_like(entering))
    )
    is_last = section_index == section_count - 1
    last_weight = is_last.astype(jnp.float32)
    factor = 1.0 / (micro_count * slot_count)
    loss_term, seeds, head_term = head_terms(final, target_maps[0], live, head_weight, factor)
    head_total, loss_total = lax.psum(
        (head_term * last_weight, loss_term * last_weight), ("section", "dp")
    )
    first_back, second_back = (
        lax.all_gather(weight_in[0], "dp", axis=0, tiled=True),
        lax.all_gather(weight_out[0], "dp", axis=0, tiled=True),
    )
    width = entering.shape[-1]
    expand = first_back.shape[1]
    extra_start = (jnp.zeros((width, expand), jnp.float32), jnp.zeros((expand, width), jnp.float32))

    def backward_step(moment, carry):
        arrived, kernel_acc, extra = carry
        micro = moment - (section_count - 1 - section_index)
        active = (micro >= 0) & (micro < micro_count)
        place = jnp.clip(micro, 0, micro_count - 1)
        own_seed = lax.dynamic_index_in_dim(seeds, place, 0, keepdims=False)
        upstream = jnp.where(is_last, own_seed, arrived)
        stored = lax.dynamic_index_in_dim(saved, place, 0, keepdims=False)

        def run_block(operands):
            grad_tiles, inputs, acc_kernel, acc_extra = operands
            tile_grad, kernel_term, normed_low, hidden_grad, activated, up_flat = block_backward(
                inputs, grad_tiles, kernel, first_back, second_back
            )
            new_extra = (
                acc_extra[0] + outer_sum(normed_low, hidden_grad),
                acc_extra[1] + outer_sum(activated, up_flat),
            )
            return (tile_grad, acc_kernel + kernel_term, new_extra)

        def skip_block(operands):
            return (jnp.zeros_like(operands[0]), operands[2], operands[3])

        tile_grad, kernel_acc, extra = lax.cond(
            active, run_block, skip_block, (upstream, stored, kernel_acc, extra)
        )
        arrived = from_behind(tile_grad, "section", -1)
        return (arrived, kernel_acc, extra)

    _, kernel_acc, extra = lax.fori_loop(
        0, ticks, backward_step, (blank_tile, jnp.zeros(kernel.shape, jnp.float32), extra_start)
    )
    first_part, second_part = (
        lax.psum_scatter(
            extra[0].astype(jnp.bfloat16), "dp", scatter_dimension=0, tiled=True
        ).astype(jnp.float32),
        lax.psum_scatter(
            extra[1].astype(jnp.bfloat16), "dp", scatter_dimension=0, tiled=True
        ).astype(jnp.float32),
    )
    kernel_total = lax.psum(kernel_acc.astype(jnp.bfloat16), "dp").astype(jnp.float32)
    return (first_part[None], second_part[None], kernel_total[None], head_total, loss_total)


def solution(mesh):
    return jax.shard_map(
        body,
        mesh=mesh,
        in_specs=(
            P("dp", None, None, None, None, None),
            P("dp", None, None, None, None),
            P("dp", None),
            P("section", None, None),
            P("section", "dp", None),
            P("section", "dp", None),
            P(),
        ),
        out_specs=(
            P("section", "dp", None),
            P("section", "dp", None),
            P("section", None, None),
            P(),
            P(),
        ),
        check_vma=False,
    )
```

profile of v0, /device:TPU:1, one launch (start us, length us, event | category | flops | bytes accessed | tf_op | source)
XLA Modules:
  0.0 1533.0 jit_solution(5656709828315738469)
XLA Ops:
  13.1 91.3 %all-gather.5.cloned.1.call-done = bf16[1,640,2560]{2,0,1:T(2,128)(2,1)} async-done(((bf16[1,20,2560]{2,0,1:T(2,128)(2,1)}), bf16[1,640,2560]{2,0,1:T(2,128)(2,1)}) %all-gather.5.cloned.1.call-update) | async-done | bytes 3276816 | tf_op jit(solution)/shard_map/all_gather | solution.py:135
  108.0 72.7 %all-gather.7.cloned.1.call-done = bf16[1,2560,640]{2,1,0:T(8,128)(2,1)} async-done(((bf16[1,80,640]{2,1,0:T(8,128)(2,1)}), bf16[1,2560,640]{2,1,0:T(8,128)(2,1)}) %all-gather.7.cloned.1.call-update) | async-done | bytes 3276816 | tf_op jit(solution)/shard_map/all_gather | solution.py:136
  183.2 210.7 %while.40 = (s32[]{:T(128)}, bf16[2,8,8,640]{3,2,1,0:T(8,128)(2,1)}, bf16[4,2,8,8,640]{4,3,2,1,0:T(8,128)(2,1)}, bf16[4,2,8,8,640]{4,3,2,1,0:T(8,128)(2,1)}, s32...) while((s32[]{:T(128)}, ...), condition=%wide.region_5.6_spmd, body=%wide.region_0.5_spmd.sunk | while | flops 849510528 | bytes 13491009 | solution.py:165
  195.4 12.2 collective-permute-done
  210.3 14.7 conditional.5
  231.9 14.7 conditional.5
  256.1 14.7 conditional.5
  280.3 14.7 conditional.5
  304.5 19.2 %collective-permute-start = (bf16[2,8,8,640]{3,2,1,0:T(8,128)(2,1)S(1)}, bf16[2,8,8,640]{3,2,1,0:T(8,128)(2,1)}, u32[]{:S(2)}, u32[]{:S(2)}) collective-permute-start(bf16[2,8,8,640]{3,2,1,0:T(8,128)(2,1)S(1)} %get-tuple-element.1153), channel_id=1, source_target_pairs={{0,32},{32,64},{64,96},{96,128},{128,160},{160,192},{192,224},{1,3... | collective-permute-start | bytes 491528 | tf_op jit(solution)/shard_map/while/body/eval_jaxpr/ppermute | solution.py:14
  338.2 12.7 collective-permute-start
  365.5 16.6 %collective-permute-start = (bf16[2,8,8,640]{3,2,1,0:T(8,128)(2,1)S(1)}, bf16[2,8,8,640]{3,2,1,0:T(8,128)(2,1)}, u32[]{:S(2)}, u32[]{:S(2)}) collective-permute-start(bf16[2,8,8,640]{3,2,1,0:T(8,128)(2,1)S(1)} %get-tuple-element.1153), channel_id=1, source_target_pairs={{0,32},{32,64},{64,96},{96,128},{128,160},{160,192},{192,224},{1,3... | collective-permute-start | bytes 491528 | tf_op jit(solution)/shard_map/while/body/eval_jaxpr/ppermute | solution.py:14
  403.2 778.2 %while.41 = (s32[]{:T(128)}, bf16[2,8,8,640]{3,2,1,0:T(8,128)(2,1)}, f32[49,640]{1,0:T(8,128)S(1)}, f32[640,2560]{1,0:T(8,128)}, f32[2560,640]{1,0:T(8,128)}, /*...) while((s32[]{:T(128)}, ...), condition=%wide.region_63.64_spmd.clone, body=%wide.region_7.63_spmd.clone.sunk | while | flops 2131804288 | bytes 130983528 | solution.py:212
  407.5 14.1 collective-permute-done.1
  435.2 17.3 %collective-permute-done.1 = bf16[2,8,8,640]{3,2,1,0:T(8,128)(2,1)} collective-permute-done((bf16[2,8,8,640]{3,2,1,0:T(8,128)(2,1)}, bf16[2,8,8,640]{3,2,1,0:T(8,128)(2,1)}, u32[]{:S(2)}, u32[]{:S(2)}) %collective-permute-start.1) | collective-permute-done | bytes 163872 | tf_op jit(solution)/shard_map/while/body/eval_jaxpr/ppermute | solution.py:14
  466.1 13.4 collective-permute-done.1
  483.8 359.0 %collective-permute-done.1 = bf16[2,8,8,640]{3,2,1,0:T(8,128)(2,1)} collective-permute-done((bf16[2,8,8,640]{3,2,1,0:T(8,128)(2,1)}, bf16[2,8,8,640]{3,2,1,0:T(8,128)(2,1)}, u32[]{:S(2)}, u32[]{:S(2)}) %collective-permute-start.1) | collective-permute-done | bytes 163872 | tf_op jit(solution)/shard_map/while/body/eval_jaxpr/ppermute | solution.py:14
  844.6 60.5 %conditional.6 = (bf16[2,8,8,640]{3,2,1,0:T(8,128)(2,1)}, f32[49,640]{1,0:T(8,128)S(1)}, f32[640,2560]{1,0:T(8,128)}, f32[2560,640]{1,0:T(8,128)}) conditional(s32[]{:T(128)} %convert_element_type.175, (f32[49,640]{1,0:T(8,128)S(1)}, f32[640,2560]{1,0:T(8,128)}, f32[2560,640]{1,0:T(8,128)}) %tuple.251, (pred[]{:T(512)}, s32[]{:T(128)}, ...), branch_computations={%region_8.8_spmd, %region_9.62_spmd} | conditional | flops 2131148928 | bytes 129667864 | solution.py:206
  913.7 60.5 %conditional.6 = (bf16[2,8,8,640]{3,2,1,0:T(8,128)(2,1)}, f32[49,640]{1,0:T(8,128)S(1)}, f32[640,2560]{1,0:T(8,128)}, f32[2560,640]{1,0:T(8,128)}) conditional(s32[]{:T(128)} %convert_element_type.175, (f32[49,640]{1,0:T(8,128)S(1)}, f32[640,2560]{1,0:T(8,128)}, f32[2560,640]{1,0:T(8,128)}) %tuple.251, (pred[]{:T(512)}, s32[]{:T(128)}, ...), branch_computations={%region_8.8_spmd, %region_9.62_spmd} | conditional | flops 2131148928 | bytes 129667864 | solution.py:206
  982.8 60.5 %conditional.6 = (bf16[2,8,8,640]{3,2,1,0:T(8,128)(2,1)}, f32[49,640]{1,0:T(8,128)S(1)}, f32[640,2560]{1,0:T(8,128)}, f32[2560,640]{1,0:T(8,128)}) conditional(s32[]{:T(128)} %convert_element_type.175, (f32[49,640]{1,0:T(8,128)S(1)}, f32[640,2560]{1,0:T(8,128)}, f32[2560,640]{1,0:T(8,128)}) %tuple.251, (pred[]{:T(512)}, s32[]{:T(128)}, ...), branch_computations={%region_8.8_spmd, %region_9.62_spmd} | conditional | flops 2131148928 | bytes 129667864 | solution.py:206
  1051.9 60.5 %conditional.6 = (bf16[2,8,8,640]{3,2,1,0:T(8,128)(2,1)}, f32[49,640]{1,0:T(8,128)S(1)}, f32[640,2560]{1,0:T(8,128)}, f32[2560,640]{1,0:T(8,128)}) conditional(s32[]{:T(128)} %convert_element_type.175, (f32[49,640]{1,0:T(8,128)S(1)}, f32[640,2560]{1,0:T(8,128)}, f32[2560,640]{1,0:T(8,128)}) %tuple.251, (pred[]{:T(512)}, s32[]{:T(128)}, ...), branch_computations={%region_8.8_spmd, %region_9.62_spmd} | conditional | flops 2131148928 | bytes 129667864 | solution.py:206
  1121.6 58.4 %collective-permute-start.1 = (bf16[2,8,8,640]{3,2,1,0:T(8,128)(2,1)}, bf16[2,8,8,640]{3,2,1,0:T(8,128)(2,1)}, u32[]{:S(2)}, u32[]{:S(2)}) collective-permute-start(bf16[2,8,8,640]{3,2,1,0:T(8,128)(2,1)} %get-tuple-element.1051), channel_id=1, source_target_pairs={{32,0},{64,32},{96,64},{128,96},{160,128},{192,160},{224,192},{33,... | collective-permute-start | bytes 491528 | tf_op jit(solution)/shard_map/while/body/eval_jaxpr/ppermute | solution.py:14
  1191.4 84.2 %fusion.2 = bf16[24,2560]{1,0:T(8,128)(2,1)} fusion(bf16[640,2560]{1,0:T(8,128)(2,1)S(1)} %convert_element_type.133), kind=kCustom, calls=%all-reduce-scatter | all-reduce-scatter fusion | flops 1966081 | bytes 3400704
  1294.3 110.5 %psum.21 = bf16[1,49,640]{2,0,1:T(2,128)(2,1)S(1)} all-reduce(bf16[1,49,640]{2,0,1:T(2,128)(2,1)S(1)} %broadcast_in_dim.64), channel_id=1, replica_groups=mesh['section'=8,'dp'=32] {'dp'}, use_global_device_ids=true, to_apply=%region_66.67 | all-reduce | flops 31360 | bytes 125440 | tf_op jit(solution)/shard_map/psum | solution.py:223
  1406.9 115.7 %all-reduce.5 = (f32[640]{0:T(1024)}, f32[]{:T(128)}) all-reduce(f32[640]{0:T(1024)S(1)} %broadcast_multiply_fusion.4, f32[]{:T(128)S(6)} %mul.2377), channel_id=1, replica_groups=mesh['section'=8,'dp'=32] {'section','dp'}, use_global_device_ids=true, to_apply=%region_68.69 | all-reduce | flops 641 | bytes 5128 | tf_op jit(solution)/shard_map/psum | solution.py:172
  (1176 shorter events, 519.7 us)
Async XLA Ops:
  7.2 97.2 %all-gather.5.cloned.1.call-start = ((), (), s32[]{:S(2)}) async-start(), calls=%async_computation.2 | async-start | bytes 6758400 | tf_op jit(solution)/shard_map/all_gather | solution.py:135
  9.0 171.6 %all-gather.7.cloned.1.call-start = ((), (), s32[]{:S(2)}) async-start(), calls=%async_computation.3 | async-start | bytes 3379200 | tf_op jit(solution)/shard_map/all_gather | solution.py:136
  9.8 1515.1 %reduce-scatter.4.cloned.1.call-start = ((), (), s32[]{:S(2)}) async-start(), calls=%async_computation.1 | async-start | bytes 3379200 | tf_op jit(solution)/shard_map/reduce_scatter | solution.py:219
  185.9 21.6 %collective-permute-start = (bf16[2,8,8,640]{3,2,1,0:T(8,128)(2,1)S(1)}, bf16[2,8,8,640]{3,2,1,0:T(8,128)(2,1)}, u32[]{:S(2)}, u32[]{:S(2)}) collective-permute-start(bf16[2,8,8,640]{3,2,1,0:T(8,128)(2,1)S(1)} %get-tuple-element.1153), channel_id=1, source_target_pairs={{0,32},{32,64},{64,96},{96,128},{128,160},{160,192},{192,224},{1,3... | collective-permute-start | bytes 491528 | tf_op jit(solution)/shard_map/while/body/eval_jaxpr/ppermute | solution.py:14
  304.5 21.4 %collective-permute-start = (bf16[2,8,8,640]{3,2,1,0:T(8,128)(2,1)S(1)}, bf16[2,8,8,640]{3,2,1,0:T(8,128)(2,1)}, u32[]{:S(2)}, u32[]{:S(2)}) collective-permute-start(bf16[2,8,8,640]{3,2,1,0:T(8,128)(2,1)S(1)} %get-tuple-element.1153), channel_id=1, source_target_pairs={{0,32},{32,64},{64,96},{96,128},{128,160},{160,192},{192,224},{1,3... | collective-permute-start | bytes 491528 | tf_op jit(solution)/shard_map/while/body/eval_jaxpr/ppermute | solution.py:14
  338.2 14.9 collective-permute-start
  365.5 18.8 %collective-permute-start = (bf16[2,8,8,640]{3,2,1,0:T(8,128)(2,1)S(1)}, bf16[2,8,8,640]{3,2,1,0:T(8,128)(2,1)}, u32[]{:S(2)}, u32[]{:S(2)}) collective-permute-start(bf16[2,8,8,640]{3,2,1,0:T(8,128)(2,1)S(1)} %get-tuple-element.1153), channel_id=1, source_target_pairs={{0,32},{32,64},{64,96},{96,128},{128,160},{160,192},{192,224},{1,3... | collective-permute-start | bytes 491528 | tf_op jit(solution)/shard_map/while/body/eval_jaxpr/ppermute | solution.py:14
  405.6 16.0 %collective-permute-start.1 = (bf16[2,8,8,640]{3,2,1,0:T(8,128)(2,1)}, bf16[2,8,8,640]{3,2,1,0:T(8,128)(2,1)}, u32[]{:S(2)}, u32[]{:S(2)}) collective-permute-start(bf16[2,8,8,640]{3,2,1,0:T(8,128)(2,1)} %get-tuple-element.1051), channel_id=1, source_target_pairs={{32,0},{64,32},{96,64},{128,96},{160,128},{192,160},{224,192},{33,... | collective-permute-start | bytes 491528 | tf_op jit(solution)/shard_map/while/body/eval_jaxpr/ppermute | solution.py:14
  423.9 6.9 collective-permute-start.1
  433.3 19.2 %collective-permute-start.1 = (bf16[2,8,8,640]{3,2,1,0:T(8,128)(2,1)}, bf16[2,8,8,640]{3,2,1,0:T(8,128)(2,1)}, u32[]{:S(2)}, u32[]{:S(2)}) collective-permute-start(bf16[2,8,8,640]{3,2,1,0:T(8,128)(2,1)} %get-tuple-element.1051), channel_id=1, source_target_pairs={{32,0},{64,32},{96,64},{128,96},{160,128},{192,160},{224,192},{33,... | collective-permute-start | bytes 491528 | tf_op jit(solution)/shard_map/while/body/eval_jaxpr/ppermute | solution.py:14
  454.9 6.9 collective-permute-start.1
  464.2 15.3 %collective-permute-start.1 = (bf16[2,8,8,640]{3,2,1,0:T(8,128)(2,1)}, bf16[2,8,8,640]{3,2,1,0:T(8,128)(2,1)}, u32[]{:S(2)}, u32[]{:S(2)}) collective-permute-start(bf16[2,8,8,640]{3,2,1,0:T(8,128)(2,1)} %get-tuple-element.1051), channel_id=1, source_target_pairs={{32,0},{64,32},{96,64},{128,96},{160,128},{192,160},{224,192},{33,... | collective-permute-start | bytes 491528 | tf_op jit(solution)/shard_map/while/body/eval_jaxpr/ppermute | solution.py:14
  481.9 361.0 %collective-permute-start.1 = (bf16[2,8,8,640]{3,2,1,0:T(8,128)(2,1)}, bf16[2,8,8,640]{3,2,1,0:T(8,128)(2,1)}, u32[]{:S(2)}, u32[]{:S(2)}) collective-permute-start(bf16[2,8,8,640]{3,2,1,0:T(8,128)(2,1)} %get-tuple-element.1051), channel_id=1, source_target_pairs={{32,0},{64,32},{96,64},{128,96},{160,128},{192,160},{224,192},{33,... | collective-permute-start | bytes 491528 | tf_op jit(solution)/shard_map/while/body/eval_jaxpr/ppermute | solution.py:14
  905.0 6.9 collective-permute-start.1
  974.1 6.9 collective-permute-start.1
  1043.2 6.9 collective-permute-start.1
  1112.3 6.9 collective-permute-start.1
  1121.6 59.7 %collective-permute-start.1 = (bf16[2,8,8,640]{3,2,1,0:T(8,128)(2,1)}, bf16[2,8,8,640]{3,2,1,0:T(8,128)(2,1)}, u32[]{:S(2)}, u32[]{:S(2)}) collective-permute-start(bf16[2,8,8,640]{3,2,1,0:T(8,128)(2,1)} %get-tuple-element.1051), channel_id=1, source_target_pairs={{32,0},{64,32},{96,64},{128,96},{160,128},{192,160},{224,192},{33,... | collective-permute-start | bytes 491528 | tf_op jit(solution)/shard_map/while/body/eval_jaxpr/ppermute | solution.py:14
  1276.5 246.1 %collective-permute-start.6 = (bf16[24,2560]{1,0:T(8,128)(2,1)}, bf16[24,2560]{1,0:T(8,128)(2,1)S(1)}, u32[]{:S(2)}, u32[]{:S(2)}) collective-permute-start(bf16[24,2560]{1,0:T(8,128)(2,1)} %fusion.2), channel_id=1, source_target_pairs={{0,5},{1,6},{2,7},{3,8},{4,9},{5,10},{6,11},{7,12},{8,13},{9,14},{... | collective-permute-start | bytes 368648
  1277.8 244.8 %collective-permute-start.5 = (bf16[24,2560]{1,0:T(8,128)(2,1)}, bf16[24,2560]{1,0:T(8,128)(2,1)S(1)}, u32[]{:S(2)}, u32[]{:S(2)}) collective-permute-start(bf16[24,2560]{1,0:T(8,128)(2,1)} %fusion.2), channel_id=1, source_target_pairs={{0,4},{1,5},{2,6},{3,7},{4,8},{5,9},{6,10},{7,11},{8,12},{9,13},{1... | collective-permute-start | bytes 368648
  1279.3 243.3 %collective-permute-start.4 = (bf16[24,2560]{1,0:T(8,128)(2,1)}, bf16[24,2560]{1,0:T(8,128)(2,1)S(1)}, u32[]{:S(2)}, u32[]{:S(2)}) collective-permute-start(bf16[24,2560]{1,0:T(8,128)(2,1)} %fusion.2), channel_id=1, source_target_pairs={{0,3},{1,4},{2,5},{3,6},{4,7},{5,8},{6,9},{7,10},{8,11},{9,12},{10... | collective-permute-start | bytes 368648
  1280.6 242.0 %collective-permute-start.3 = (bf16[24,2560]{1,0:T(8,128)(2,1)}, bf16[24,2560]{1,0:T(8,128)(2,1)S(1)}, u32[]{:S(2)}, u32[]{:S(2)}) collective-permute-start(bf16[24,2560]{1,0:T(8,128)(2,1)} %fusion.2), channel_id=1, source_target_pairs={{0,2},{1,3},{2,4},{3,5},{4,6},{5,7},{6,8},{7,9},{8,10},{9,11},{10,... | collective-permute-start | bytes 368648
  1283.4 122.2 %collective-permute-start.7 = (bf16[4,2560]{1,0:T(4,128)(2,1)S(1)}, bf16[4,2560]{1,0:T(4,128)(2,1)S(1)}, u32[]{:S(2)}, u32[]{:S(2)}) collective-permute-start(bf16[4,2560]{1,0:T(4,128)(2,1)S(1)} %slice.1262), channel_id=1, source_target_pairs={{0,6},{1,7},{2,8},{3,9},{4,10},{5,11},{6,12},{7,13},{8,14},{9,15},... | collective-permute-start | bytes 61448
  1405.6 117.0 %collective-permute-start.2 = (bf16[24,2560]{1,0:T(8,128)(2,1)S(1)}, bf16[24,2560]{1,0:T(8,128)(2,1)S(1)}, u32[]{:S(2)}, u32[]{:S(2)}) collective-permute-start(bf16[24,2560]{1,0:T(8,128)(2,1)S(1)} %copy-done.77), channel_id=1, source_target_pairs={{0,1},{1,2},{2,3},{3,4},{4,5},{5,6},{6,7},{7,8},{8,9},{9,10},{10,1... | collective-permute-start | bytes 368648
  (339 other events, 1249.0 us)
Sparse Core Ops, SparseCore 0:
  11.2 93.1 all-gather.4
  107.0 73.6 all-gather.6
  1186.4 193.5 reduce-scatter.3
where the time goes:
time: 1540 us; the launch traced here: 1530 us
  waiting for transfers between devices  618 us (40%)
  blocking collectives  310 us (20%)
  local copies, waits for them, and re-layouts  199 us (13%)
  starting transfers between devices  180 us (12%)
  other arithmetic  145 us (9%)
  matrix products  59.4 us (4%)
    ppermute x22, waiting for transfers between devices, from_behind(): lax.ppermute(value, axis, [(source, source + steps) for source in range(f...  453 us
    ppermute x22, starting transfers between devices, from_behind(): lax.ppermute(value, axis, [(source, source + steps) for source in range(f...  163 us
    psum x1, blocking collectives, body(): lax.psum((head_term * last_weight, loss_term * last_weight), ('section',...  116 us
    psum x1, blocking collectives, body(): lax.psum(kernel_acc.astype(jnp.bfloat16), 'dp').astype(jnp.float32)  111 us
    another operation x200, local copies, waits for them, and re-layouts, kernel_grad(): return jnp.stack(taps, axis=0)  105 us
    all_gather x1, waiting for transfers between devices, body(): lax.all_gather(weight_in[0], 'dp', axis=0, tiled=True)  91.3 us
    unnamed x1, blocking collectives  84.2 us
    all_gather x1, waiting for transfers between devices, body(): lax.all_gather(weight_out[0], 'dp', axis=0, tiled=True)  72.7 us
  transfers between devices with their start and end apart: 31, of which 24 were waited for; matrix products, arithmetic and copies ran while one was open for 8% of the time, Pallas kernels for 0%

commit v1 on v0

--- a/solution.py
+++ b/solution.py
@@ -132,7 +132,9 @@
     live = jnp.arange(slot_count)[None, :] < crop_counts[0][:, None]
     entering = crop_maps[0] * live[:, :, None, None, None].astype(jnp.bfloat16)
     first_full, second_full = (
-        lax.all_gather(weight_in[0], "dp", axis=0, tiled=True),
+        jnp.concatenate(
+            lax.all_to_all(jnp.stack([weight_in[0]] * lax.axis_size("dp")), "dp", 0, 0), axis=0
+        ),
         lax.all_gather(weight_out[0], "dp", axis=0, tiled=True),
     )
     blank_tile = jnp.zeros(entering.shape[1:], jnp.bfloat16)

time: 1540 us -> 1380 us (0.90)
  waiting for transfers between devices: 618 us -> 548 us
  other arithmetic: 145 us -> 101 us
  local copies, waits for them, and re-layouts: 199 us -> 166 us
    all_to_all x0 -> x1, waiting for transfers between devices: none -> 105 us  [body(): lax.all_to_all(jnp.stack([weight_in[0]] * lax.axis_size('dp')), 'dp', 0, 0)]
    all_gather x1, waiting for transfers between devices: 91.3 us -> 0.01 us  [body(): lax.all_gather(weight_in[0], 'dp', axis=0, tiled=True)]
    all_gather x1, waiting for transfers between devices: 72.7 us -> 0.01 us  [body(): lax.all_gather(weight_out[0], 'dp', axis=0, tiled=True)]
    ppermute x22, starting transfers between devices: 163 us -> 138 us  [from_behind(): lax.ppermute(value, axis, [(source, source + steps) for source in range(f...]
    dynamic_update_slice x11, other arithmetic: 19.9 us -> 1.11 us  [forward_step(): lax.dynamic_update_index_in_dim(saved, jnp.where(active, current, old_sav...]
  transfers between devices with their start and end apart: 31 -> 32, of which waited for: 24 -> 23; matrix products, arithmetic and copies ran while one was open for 8% -> 10% of each run, Pallas kernels for 0% -> 0%
where the time goes in v1:
time: 1380 us
  waiting for transfers between devices  548 us (40%)
  blocking collectives  306 us (22%)
  starting transfers between devices  169 us (12%)
  local copies, waits for them, and re-layouts  166 us (12%)
  other arithmetic  101 us (7%)
  matrix products  63.2 us (5%)
  between operations  15.3 us (1%)
    ppermute x22, waiting for transfers between devices, from_behind(): lax.ppermute(value, axis, [(source, source + steps) for source in range(f...  442 us
    ppermute x22, starting transfers between devices, from_behind(): lax.ppermute(value, axis, [(source, source + steps) for source in range(f...  138 us
    psum x1, blocking collectives, body(): lax.psum((head_term * last_weight, loss_term * last_weight), ('section',...  113 us
    psum x1, blocking collectives, body(): lax.psum(kernel_acc.astype(jnp.bfloat16), 'dp').astype(jnp.float32)  111 us
    all_to_all x1, waiting for transfers between devices, body(): lax.all_to_all(jnp.stack([weight_in[0]] * lax.axis_size('dp')), 'dp', 0, 0)  105 us
    another operation x200, local copies, waits for them, and re-layouts, kernel_grad(): return jnp.stack(taps, axis=0)  105 us
    unnamed x1, blocking collectives  82.2 us
    dot_general x8, matrix products, outer_sum(): lax.dot_general(left, right, (((0,), (0,)), ((), ())), preferred_element_...  33.9 us
  transfers between devices with their start and end apart: 32, of which 23 were waited for; matrix products, arithmetic and copies ran while one was open for 10% of the time, Pallas kernels for 0%

profile of v1, /device:TPU:1, one launch (start us, length us, event | category | flops | bytes accessed | tf_op | source)
XLA Modules:
  0.0 1375.9 jit_solution(6134945424883400815)
XLA Ops:
  11.1 12.1 all-to-all-start
  24.4 105.3 %all-to-all-done = bf16[32,20,2560]{2,1,0:T(8,128)(2,1)} async-done(((bf16[32,20,2560]{2,1,0:T(8,128)(2,1)}), bf16[32,20,2560]{2,1,0:T(8,128)(2,1)}, u32[]{:S(2)}, u32[]{:S(2)}) %all-to-all-start) | async-done | bytes 3276832 | tf_op jit(solution)/shard_map/all_to_all | solution.py:136
  135.4 121.2 %while.40 = (s32[]{:T(128)}, bf16[2,8,8,640]{3,2,1,0:T(8,128)(2,1)S(1)}, bf16[4,2,8,8,640]{4,3,2,1,0:T(8,128)(2,1)S(1)}, bf16[4,2,8,8,640]{4,3,2,1,0:T(8,128)(2,...) while((s32[]{:T(128)}, ...), condition=%wide.region_5.6_spmd, body=%wide.region_0.5_spmd.sunk | while | flops 849510528 | bytes 12179750 | solution.py:167
  147.9 7.6 conditional.5
  159.8 7.6 conditional.5
  188.4 7.6 conditional.5
  202.8 12.0 collective-permute-start
  238.0 9.6 collective-permute-start
  269.3 756.9 %while.41 = (s32[]{:T(128)}, bf16[2,8,8,640]{3,2,1,0:T(8,128)(2,1)}, f32[49,640]{1,0:T(8,128)S(1)}, f32[640,2560]{1,0:T(8,128)}, f32[2560,640]{1,0:T(8,128)}, /*...) while((s32[]{:T(128)}, ...), condition=%wide.region_63.64_spmd.clone, body=%wide.region_7.63_spmd.clone.sunk | while | flops 2131804288 | bytes 130983528 | solution.py:214
  293.4 10.7 collective-permute-done.1
  328.1 359.6 %collective-permute-done.1 = bf16[2,8,8,640]{3,2,1,0:T(8,128)(2,1)} collective-permute-done((bf16[2,8,8,640]{3,2,1,0:T(8,128)(2,1)}, bf16[2,8,8,640]{3,2,1,0:T(8,128)(2,1)}, u32[]{:S(2)}, u32[]{:S(2)}) %collective-permute-start.1) | collective-permute-done | bytes 163872 | tf_op jit(solution)/shard_map/while/body/eval_jaxpr/ppermute | solution.py:14
  689.4 60.5 %conditional.6 = (bf16[2,8,8,640]{3,2,1,0:T(8,128)(2,1)}, f32[49,640]{1,0:T(8,128)S(1)}, f32[640,2560]{1,0:T(8,128)}, f32[2560,640]{1,0:T(8,128)}) conditional(s32[]{:T(128)} %convert_element_type.175, (f32[49,640]{1,0:T(8,128)S(1)}, f32[640,2560]{1,0:T(8,128)}, f32[2560,640]{1,0:T(8,128)}) %tuple.251, (pred[]{:T(512)}, s32[]{:T(128)}, ...), branch_computations={%region_8.8_spmd, %region_9.62_spmd} | conditional | flops 2131148928 | bytes 129667864 | solution.py:208
  728.9 8.0 stack.301
  758.5 60.5 %conditional.6 = (bf16[2,8,8,640]{3,2,1,0:T(8,128)(2,1)}, f32[49,640]{1,0:T(8,128)S(1)}, f32[640,2560]{1,0:T(8,128)}, f32[2560,640]{1,0:T(8,128)}) conditional(s32[]{:T(128)} %convert_element_type.175, (f32[49,640]{1,0:T(8,128)S(1)}, f32[640,2560]{1,0:T(8,128)}, f32[2560,640]{1,0:T(8,128)}) %tuple.251, (pred[]{:T(512)}, s32[]{:T(128)}, ...), branch_computations={%region_8.8_spmd, %region_9.62_spmd} | conditional | flops 2131148928 | bytes 129667864 | solution.py:208
  797.9 8.0 stack.301
  827.6 60.5 %conditional.6 = (bf16[2,8,8,640]{3,2,1,0:T(8,128)(2,1)}, f32[49,640]{1,0:T(8,128)S(1)}, f32[640,2560]{1,0:T(8,128)}, f32[2560,640]{1,0:T(8,128)}) conditional(s32[]{:T(128)} %convert_element_type.175, (f32[49,640]{1,0:T(8,128)S(1)}, f32[640,2560]{1,0:T(8,128)}, f32[2560,640]{1,0:T(8,128)}) %tuple.251, (pred[]{:T(512)}, s32[]{:T(128)}, ...), branch_computations={%region_8.8_spmd, %region_9.62_spmd} | conditional | flops 2131148928 | bytes 129667864 | solution.py:208
  867.0 8.0 stack.301
  896.7 60.5 %conditional.6 = (bf16[2,8,8,640]{3,2,1,0:T(8,128)(2,1)}, f32[49,640]{1,0:T(8,128)S(1)}, f32[640,2560]{1,0:T(8,128)}, f32[2560,640]{1,0:T(8,128)}) conditional(s32[]{:T(128)} %convert_element_type.175, (f32[49,640]{1,0:T(8,128)S(1)}, f32[640,2560]{1,0:T(8,128)}, f32[2560,640]{1,0:T(8,128)}) %tuple.251, (pred[]{:T(512)}, s32[]{:T(128)}, ...), branch_computations={%region_8.8_spmd, %region_9.62_spmd} | conditional | flops 2131148928 | bytes 129667864 | solution.py:208
  936.1 8.0 stack.301
  966.5 58.4 %collective-permute-start.1 = (bf16[2,8,8,640]{3,2,1,0:T(8,128)(2,1)}, bf16[2,8,8,640]{3,2,1,0:T(8,128)(2,1)}, u32[]{:S(2)}, u32[]{:S(2)}) collective-permute-start(bf16[2,8,8,640]{3,2,1,0:T(8,128)(2,1)} %get-tuple-element.1051), channel_id=1, source_target_pairs={{32,0},{64,32},{96,64},{128,96},{160,128},{192,160},{224,192},{33,... | collective-permute-start | bytes 491528 | tf_op jit(solution)/shard_map/while/body/eval_jaxpr/ppermute | solution.py:14
  1036.2 82.2 %fusion.2 = bf16[24,2560]{1,0:T(8,128)(2,1)} fusion(bf16[640,2560]{1,0:T(8,128)(2,1)S(1)} %convert_element_type.133), kind=kCustom, calls=%all-reduce-scatter | all-reduce-scatter fusion | flops 1966081 | bytes 3400704
  1127.0 11.3 collective-permute-start.7
  1139.6 110.7 %psum.21 = bf16[1,49,640]{2,0,1:T(2,128)(2,1)S(1)} all-reduce(bf16[1,49,640]{2,0,1:T(2,128)(2,1)S(1)} %broadcast_in_dim.64), channel_id=1, replica_groups=mesh['section'=8,'dp'=32] {'dp'}, use_global_device_ids=true, to_apply=%region_66.67 | all-reduce | flops 31360 | bytes 125440 | tf_op jit(solution)/shard_map/psum | solution.py:225
  1252.4 113.0 %all-reduce.5 = (f32[640]{0:T(1024)}, f32[]{:T(128)}) all-reduce(f32[640]{0:T(1024)S(1)} %broadcast_multiply_fusion.4, f32[]{:T(128)S(6)} %mul.2377), channel_id=1, replica_groups=mesh['section'=8,'dp'=32] {'section','dp'}, use_global_device_ids=true, to_apply=%region_68.69 | all-reduce | flops 641 | bytes 5128 | tf_op jit(solution)/shard_map/psum | solution.py:174
  (1184 shorter events, 450.3 us)
Async XLA Ops:
  7.2 128.1 %all-gather.5.cloned.1.call-start = ((), (), s32[]{:S(2)}) async-start(), calls=%async_computation.3 | async-start | bytes 3379200 | tf_op jit(solution)/shard_map/all_gather | solution.py:138
  11.1 118.7 %all-to-all-start = ((bf16[32,20,2560]{2,1,0:T(8,128)(2,1)}), bf16[32,20,2560]{2,1,0:T(8,128)(2,1)}, u32[]{:S(2)}, u32[]{:S(2)}) async-start(bf16[32,20,2560]{2,1,0:T(8,128)(2,1)} %stack.303), calls=%async_computation | async-start | bytes 7864320 | tf_op jit(solution)/shard_map/all_to_all | solution.py:136
  23.2 235.1 %all-gather.7.cloned.1.call-start = ((), (), s32[]{:S(2)}) async-start(), calls=%async_computation.4 | async-start | bytes 6758400 | tf_op jit(solution)/shard_map/all_gather | solution.py:178
  24.1 1343.7 %reduce-scatter.4.cloned.1.call-start = ((), (), s32[]{:S(2)}) async-start(), calls=%async_computation.2 | async-start | bytes 3379200 | tf_op jit(solution)/shard_map/reduce_scatter | solution.py:221
  135.6 12.1 collective-permute-start
  202.8 14.2 %collective-permute-start = (bf16[2,8,8,640]{3,2,1,0:T(8,128)(2,1)S(1)}, bf16[2,8,8,640]{3,2,1,0:T(8,128)(2,1)S(1)}, u32[]{:S(2)}, u32[]{:S(2)}) collective-permute-start(bf16[2,8,8,640]{3,2,1,0:T(8,128)(2,1)S(1)} %get-tuple-element.1153), channel_id=1, source_target_pairs={{0,32},{32,64},{64,96},{96,128},{128,160},{160,192},{192,224},{1,3... | collective-permute-start | bytes 491528 | tf_op jit(solution)/shard_map/while/body/eval_jaxpr/ppermute | solution.py:14
  224.0 7.1 collective-permute-start
  238.0 11.8 collective-permute-start
  271.7 8.1 collective-permute-start.1
  282.2 6.9 collective-permute-start.1
  291.5 12.6 collective-permute-start.1
  315.8 8.0 collective-permute-start.1
  326.2 361.5 %collective-permute-start.1 = (bf16[2,8,8,640]{3,2,1,0:T(8,128)(2,1)}, bf16[2,8,8,640]{3,2,1,0:T(8,128)(2,1)}, u32[]{:S(2)}, u32[]{:S(2)}) collective-permute-start(bf16[2,8,8,640]{3,2,1,0:T(8,128)(2,1)} %get-tuple-element.1051), channel_id=1, source_target_pairs={{32,0},{64,32},{96,64},{128,96},{160,128},{192,160},{224,192},{33,... | collective-permute-start | bytes 491528 | tf_op jit(solution)/shard_map/while/body/eval_jaxpr/ppermute | solution.py:14
  749.9 6.9 collective-permute-start.1
  819.0 6.9 collective-permute-start.1
  888.1 6.9 collective-permute-start.1
  957.2 6.9 collective-permute-start.1
  966.5 59.7 %collective-permute-start.1 = (bf16[2,8,8,640]{3,2,1,0:T(8,128)(2,1)}, bf16[2,8,8,640]{3,2,1,0:T(8,128)(2,1)}, u32[]{:S(2)}, u32[]{:S(2)}) collective-permute-start(bf16[2,8,8,640]{3,2,1,0:T(8,128)(2,1)} %get-tuple-element.1051), channel_id=1, source_target_pairs={{32,0},{64,32},{96,64},{128,96},{160,128},{192,160},{224,192},{33,... | collective-permute-start | bytes 491528 | tf_op jit(solution)/shard_map/while/body/eval_jaxpr/ppermute | solution.py:14
  1119.3 246.2 %collective-permute-start.6 = (bf16[24,2560]{1,0:T(8,128)(2,1)}, bf16[24,2560]{1,0:T(8,128)(2,1)S(1)}, u32[]{:S(2)}, u32[]{:S(2)}) collective-permute-start(bf16[24,2560]{1,0:T(8,128)(2,1)} %fusion.2), channel_id=1, source_target_pairs={{0,5},{1,6},{2,7},{3,8},{4,9},{5,10},{6,11},{7,12},{8,13},{9,14},{... | collective-permute-start | bytes 368648
  1120.6 244.9 %collective-permute-start.5 = (bf16[24,2560]{1,0:T(8,128)(2,1)}, bf16[24,2560]{1,0:T(8,128)(2,1)S(1)}, u32[]{:S(2)}, u32[]{:S(2)}) collective-permute-start(bf16[24,2560]{1,0:T(8,128)(2,1)} %fusion.2), channel_id=1, source_target_pairs={{0,4},{1,5},{2,6},{3,7},{4,8},{5,9},{6,10},{7,11},{8,12},{9,13},{1... | collective-permute-start | bytes 368648
  1122.1 243.3 %collective-permute-start.4 = (bf16[24,2560]{1,0:T(8,128)(2,1)}, bf16[24,2560]{1,0:T(8,128)(2,1)S(1)}, u32[]{:S(2)}, u32[]{:S(2)}) collective-permute-start(bf16[24,2560]{1,0:T(8,128)(2,1)} %fusion.2), channel_id=1, source_target_pairs={{0,3},{1,4},{2,5},{3,6},{4,7},{5,8},{6,9},{7,10},{8,11},{9,12},{10... | collective-permute-start | bytes 368648
  1123.4 242.0 %collective-permute-start.3 = (bf16[24,2560]{1,0:T(8,128)(2,1)}, bf16[24,2560]{1,0:T(8,128)(2,1)S(1)}, u32[]{:S(2)}, u32[]{:S(2)}) collective-permute-start(bf16[24,2560]{1,0:T(8,128)(2,1)} %fusion.2), channel_id=1, source_target_pairs={{0,2},{1,3},{2,4},{3,5},{4,6},{5,7},{6,8},{7,9},{8,10},{9,11},{10,... | collective-permute-start | bytes 368648
  1127.0 124.1 %collective-permute-start.7 = (bf16[4,2560]{1,0:T(4,128)(2,1)S(1)}, bf16[4,2560]{1,0:T(4,128)(2,1)S(1)}, u32[]{:S(2)}, u32[]{:S(2)}) collective-permute-start(bf16[4,2560]{1,0:T(4,128)(2,1)S(1)} %slice.1262), channel_id=1, source_target_pairs={{0,6},{1,7},{2,8},{3,9},{4,10},{5,11},{6,12},{7,13},{8,14},{9,15},... | collective-permute-start | bytes 61448
  1251.1 114.4 %collective-permute-start.2 = (bf16[24,2560]{1,0:T(8,128)(2,1)S(1)}, bf16[24,2560]{1,0:T(8,128)(2,1)S(1)}, u32[]{:S(2)}, u32[]{:S(2)}) collective-permute-start(bf16[24,2560]{1,0:T(8,128)(2,1)S(1)} %copy-done.79), channel_id=1, source_target_pairs={{0,1},{1,2},{2,3},{3,4},{4,5},{5,6},{6,7},{7,8},{8,9},{9,10},{10,1... | collective-permute-start | bytes 368648
  (342 other events, 1217.9 us)
Sparse Core Ops, SparseCore 0:
  10.6 117.2 all-gather.4
  131.0 91.5 all-gather.6
  1031.2 194.6 reduce-scatter.3
